TPU v7x, 256 devices: a whole 4x4x8 slice. The times are simulated.
256 devices in a mesh: row: 64 (over z_hi, y, x), rep: 4 (over z_lo, core).
Axes of the slice: x: 4, y: 4, z: 8 (z_hi: 4, z_lo: 2; z = z_hi * 2 + z_lo), core: 2. Of those that a mesh axis runs over, the one named last changes fastest.
Arguments:
- features: bfloat16 [32768, 128], P('row'), may hold values from -6 to 6
- weight_one: bfloat16 [128, 128], replicated, may hold values from -0.5 to 0.5
- weight_two: bfloat16 [128, 128], replicated, may hold values from -0.5 to 0.5
- cotangent: bfloat16 [32768, 128], P('row'), may hold values from -0.03125 to 0.03125
- adj_tiles: bfloat16 [64, 64, 16, 128, 128], P('row', 'rep'), may hold values from -0.09375 to 0.09375
- tile_rows: int32 [64, 64, 16], P('row', 'rep'), may hold values from 0 to 3, as said below
- tile_cols: int32 [64, 64, 16], P('row', 'rep'), may hold values from 0 to 3
- tile_counts: int32 [64, 64], P('row', 'rep'), may hold values from 0 to 16, as said below
Outputs:
- output: bfloat16 [32768, 128], P('row')
- grad_one: float32 [128, 128], replicated
- grad_two: float32 [128, 128], replicated
Inputs may be any that keep to these rules, and one draw needn't show every extreme that they name: Only slots 0 to tile_counts[b, s] - 1 of block-row b and section s are live; the other slots carry arbitrary tiles and indices that are not part of A. Section b of block-row b holds 16 live slots; many other sections hold none. `tile_rows`: the (row, column) pairs of the slots of one block-row and section are distinct.
All inputs are finite; a program needn't handle non-finite values.
Results may differ from a plain program's by a relative error of at most 0.0065.
Values may be sent and summed in bfloat16 or wider, within the bound.
A program may use at most 192 MiB of HBM per device.

v0:
```python
from functools import partial
import jax
import jax.numpy as jnp
from jax import lax
from jax.sharding import PartitionSpec as P

TILE = 128


def gelu_value(values):
    return values * 0.5 * (1.0 + lax.erf(values * 0.7071067811865476))


def gelu_slope(values):
    normal_cdf = 0.5 * (1.0 + lax.erf(values * 0.7071067811865476))
    return normal_cdf + values * jnp.exp(-0.5 * values * values) * 0.3989422804014327


def row_contract(left, right):
    return lax.dot_general(
        left, right, (((0,), (0,)), ((), ())), preferred_element_type=jnp.float32
    )


def section_work(running, pieces, section_tiles, section_rows, section_cols, live_count):
    slot_total = section_tiles.shape[0]
    count_tiles = running.shape[0]
    sources = jnp.take(pieces, section_cols, axis=0)
    products = jnp.einsum(
        "mij,mjf->mif", section_tiles, sources, preferred_element_type=jnp.float32
    )
    live_mask = jnp.arange(slot_total, dtype=jnp.int32) < live_count
    onehot = jnp.where(
        live_mask[:, None]
        & (section_rows[:, None] == jnp.arange(count_tiles, dtype=jnp.int32)[None, :]),
        1.0,
        0.0,
    ).astype(jnp.float32)
    return running + jnp.einsum("mk,mif->kif", onehot, products, precision=lax.Precision.HIGHEST)


def propagate(tile_data, row_ids, col_ids, live_counts, own_block):
    section_total = tile_data.shape[0]
    block_rows = own_block.shape[0]
    count_tiles = block_rows // TILE
    width = own_block.shape[1]
    first_section = lax.axis_index("rep") * section_total

    def pick(section_id):
        return (
            lax.dynamic_index_in_dim(tile_data, section_id, 0, keepdims=False),
            lax.dynamic_index_in_dim(row_ids, section_id, 0, keepdims=False),
            lax.dynamic_index_in_dim(col_ids, section_id, 0, keepdims=False),
            lax.dynamic_index_in_dim(live_counts, section_id, 0, keepdims=False),
        )

    zeros = jnp.zeros((count_tiles, TILE, width), jnp.float32)
    kept_total = section_total * block_rows
    kept_base = first_section * block_rows
    empty = jnp.zeros((kept_total, width), own_block.dtype)
    piece = lax.all_gather(own_block, "row", axis=0, tiled=True)
    piece_rows = piece.shape[0]
    padding = jnp.zeros((piece_rows, width), empty.dtype)
    widened = jnp.concatenate([padding, empty, padding], axis=0)
    offset = jnp.clip(jnp.int32(0) - kept_base + piece_rows, 0, kept_total + piece_rows)
    widened = lax.dynamic_update_slice_in_dim(widened, piece, offset, 0)
    kept = widened[piece_rows : piece_rows + kept_total]
    kept = kept.reshape(section_total, count_tiles, TILE, width)

    def kept_step(section_id, running):
        pieces = lax.dynamic_index_in_dim(kept, section_id, 0, keepdims=False)
        return section_work(running, pieces, *pick(section_id))

    summed = lax.fori_loop(0, section_total, kept_step, zeros)
    return summed.reshape(block_rows, width)


def whole_sum(partial_rows):
    return lax.psum(partial_rows, "rep")


def per_device(
    features, weight_one, weight_two, cotangent, adj_tiles, tile_rows, tile_cols, tile_counts
):
    spread = partial(propagate, adj_tiles[0], tile_rows[0], tile_cols[0], tile_counts[0])
    d_two = lax.dot_general(
        cotangent, weight_two, (((1,), (1,)), ((), ())), preferred_element_type=jnp.float32
    ).astype(jnp.bfloat16)
    s_one = whole_sum(spread(features)).astype(jnp.bfloat16)
    pre_one = jnp.dot(s_one, weight_one, preferred_element_type=jnp.float32)
    hidden = gelu_value(pre_one).astype(jnp.bfloat16)
    s_two = whole_sum(spread(hidden)).astype(jnp.bfloat16)
    output = jnp.dot(s_two, weight_two, preferred_element_type=jnp.float32).astype(jnp.bfloat16)
    grad_two = lax.psum(row_contract(s_two, cotangent), "row")
    d_hidden = whole_sum(spread(d_two))
    d_pre = (d_hidden * gelu_slope(pre_one)).astype(jnp.bfloat16)
    grad_one = lax.psum(row_contract(s_one, d_pre), "row")
    return (output, grad_one, grad_two)


def solution(mesh):
    placed = (
        P("row", None),
        P(),
        P(),
        P("row", None),
        P("row", "rep", None, None, None),
        P("row", "rep", None),
        P("row", "rep", None),
        P("row", "rep"),
    )
    return jax.shard_map(
        per_device,
        mesh=mesh,
        in_specs=placed,
        out_specs=(P("row", None), P(), P()),
        check_vma=False,
    )
```

profile of v0, /device:TPU:2, one launch (start us, length us, event | category | flops | bytes accessed | tf_op | source)
XLA Modules:
  0.0 1363.7 jit_solution(14181095154365439595)
XLA Ops:
  8.1 1.6 convolution_convert_fusion
  10.6 3.9 broadcast.50
  14.4 15.8 %pad_maximum_fusion = bf16[73728,128]{1,0:T(8,128)(2,1)S(1)} fusion(bf16[32768,128]{1,0:T(8,128)(2,1)} %broadcast.50, bf16[73728]{0:T(1024)(128)(2,1)S(1)} %pad.1.clone), kind=kLoop, calls=%fused_computation.90 | loop fusion | flops 56623104 | bytes 27410432 | tf_op jit(solution)/shard_map/concatenate | solution.py:64
  30.2 6.4 copy.46
  36.6 5.8 copy-done.1
  42.4 6.5 copy.38
  48.8 73.8 %all-gather.8.cloned.1.call-done = bf16[32768,128]{1,0:T(8,128)(2,1)} async-done(((bf16[512,128]{1,0:T(8,128)(2,1)}), bf16[32768,128]{1,0:T(8,128)(2,1)}) %all-gather.8.cloned.1.call-update) | async-done | bytes 8388624 | tf_op jit(solution)/shard_map/all_gather | solution.py:61
  122.6 39.0 %dynamic_update_slice.11 = bf16[73728,128]{1,0:T(8,128)(2,1)} dynamic-update-slice(bf16[73728,128]{1,0:T(8,128)(2,1)} %copy.46, bf16[32768,128]{1,0:T(8,128)(2,1)} %all-gather.8.cloned.1.call-done, s32[]{:T(128)S(6)} %min.6, s32[]{:T(128)} %constant.163.clone.1) | dynamic-update-slice | bytes 16777220 | tf_op jit(solution)/shard_map/dynamic_update_slice | solution.py:66
  161.7 3.0 slice.20
  164.7 113.0 %while.44 = (s32[]{:T(128)}, f32[4,128,128]{2,0,1:T(4,128)S(1)}, s32[16]{0:T(128)S(1)}, s32[16,16]{1,0:T(8,128)}, bf16[16,16,128,128]{3,2,1,0:T(8,128)(2,1)}, /*...) while((s32[]{:T(128)}, f32[4,128,128]{2,0,1:T(4,128)S(1)}, ...), condition=%wide.region_7.9_spmd.clone, body=%wide.region_6.8_spmd.clone.sunk | while | flops 80086320 | bytes 4985487 | solution.py:74
  176.0 1.5 fusion.124
  183.1 1.4 fusion.124
  197.2 1.4 fusion.124
  204.3 1.4 fusion.124
  218.4 1.4 fusion.124
  232.5 1.4 fusion.124
  278.5 39.1 %dynamic_update_slice.9 = bf16[73728,128]{1,0:T(8,128)(2,1)} dynamic-update-slice(bf16[73728,128]{1,0:T(8,128)(2,1)} %copy-done.1, bf16[32768,128]{1,0:T(8,128)(2,1)} %all-gather.4.cloned.1.call-done, s32[]{:T(128)S(6)} %min.6, s32[]{:T(128)} %constant.163.clone.1) | dynamic-update-slice | bytes 16777220 | tf_op jit(solution)/shard_map/dynamic_update_slice | solution.py:66
  317.6 1.7 slice.18
  319.3 98.5 %while.42 = (s32[]{:T(128)}, f32[4,128,128]{2,0,1:T(4,128)S(1)}, s32[16]{0:T(128)S(1)}, s32[16,16]{1,0:T(8,128)}, bf16[16,16,128,128]{3,2,1,0:T(8,128)(2,1)}, /*...) while((s32[]{:T(128)}, f32[4,128,128]{2,0,1:T(4,128)S(1)}, ...), condition=%wide.region_1.3_spmd.clone, body=%wide.region_0.2_spmd.clone.sunk | while | flops 80086320 | bytes 4985487 | solution.py:74
  335.0 1.4 fusion.112
  341.1 1.4 fusion.112
  347.3 1.4 fusion.112
  417.9 21.4 %all-reduce.9 = bf16[512,128]{1,0:T(8,128)(2,1)S(1)} all-reduce(f32[512,128]{1,0:T(8,128)S(1)} %bitcast.102), channel_id=1, replica_groups=mesh['row'=64,'rep'=4] {'rep'}, use_global_device_ids=true, to_apply=%region_2.4 | all-reduce | flops 65536 | bytes 393216 | tf_op jit(solution)/shard_map/psum | solution.py:79
  440.3 1.9 fusion.69
  442.1 104.2 %all-gather.6.cloned.1.call-done = bf16[32768,128]{1,0:T(8,128)(2,1)} async-done(((bf16[512,128]{1,0:T(8,128)(2,1)}), bf16[32768,128]{1,0:T(8,128)(2,1)}) %all-gather.6.cloned.1.call-update) | async-done | bytes 8388624 | tf_op jit(solution)/shard_map/all_gather | solution.py:61
  546.3 39.1 %dynamic_update_slice.10 = bf16[73728,128]{1,0:T(8,128)(2,1)} dynamic-update-slice(bf16[73728,128]{1,0:T(8,128)(2,1)} %copy.38, bf16[32768,128]{1,0:T(8,128)(2,1)} %all-gather.6.cloned.1.call-done, s32[]{:T(128)S(6)} %min.6, s32[]{:T(128)} %constant.163.clone.1) | dynamic-update-slice | bytes 16777220 | tf_op jit(solution)/shard_map/dynamic_update_slice | solution.py:66
  585.4 1.7 slice.19
  587.2 98.5 %while.43 = (s32[]{:T(128)}, f32[4,128,128]{2,0,1:T(4,128)S(1)}, s32[16]{0:T(128)S(1)}, s32[16,16]{1,0:T(8,128)}, bf16[16,16,128,128]{3,2,1,0:T(8,128)(2,1)}, /*...) while((s32[]{:T(128)}, f32[4,128,128]{2,0,1:T(4,128)S(1)}, ...), condition=%wide.region_4.6_spmd.clone, body=%wide.region_3.5_spmd.clone.sunk | while | flops 80086320 | bytes 4985487 | solution.py:74
  685.7 21.3 %all-reduce.10 = bf16[512,128]{1,0:T(8,128)(2,1)S(1)} all-reduce(f32[512,128]{1,0:T(8,128)S(1)} %bitcast.103), channel_id=1, replica_groups=mesh['row'=64,'rep'=4] {'rep'}, use_global_device_ids=true, to_apply=%region_5.7 | all-reduce | flops 65536 | bytes 393216 | tf_op jit(solution)/shard_map/psum | solution.py:79
  708.8 645.5 %all-reduce.8.cloned.1.call-done = (f32[128,128]{1,0:T(8,128)}, f32[128,128]{1,0:T(8,128)}) async-done(((f32[128,128]{1,0:T(8,128)}, f32[128,128]{1,0:T(8,128)}), (f32[128,128]{1,0:T(8,128)}, f32[128,128]{1,0:T(8,128)})) %all-reduce.8.cloned.1.call-update) | async-done | bytes 131088 | tf_op jit(solution)/shard_map/psum | solution.py:97
  1354.2 1.5 copy.58
  1355.7 1.5 copy.59
  (457 shorter events, 300.1 us)
Async XLA Ops:
  7.2 0.9 copy-start
  7.2 115.4 %all-gather.8.cloned.1.call-start = ((), (), s32[]{:S(2)}) async-start(), calls=%async_computation.2 | async-start | bytes 8519680 | tf_op jit(solution)/shard_map/all_gather | solution.py:61
  9.7 268.8 %all-gather.4.cloned.1.call-start = ((), (), s32[]{:S(2)}) async-start(), calls=%async_computation | async-start | bytes 8519680 | tf_op jit(solution)/shard_map/all_gather | solution.py:61
  10.5 429.8 %all-reduce.6.cloned.1.call-start = ((), (), s32[]{:S(2)}) async-start(), calls=%async_computation.3 | async-start | bytes 524288 | tf_op jit(solution)/shard_map/psum | solution.py:79
  30.2 12.2 copy-start.1
  48.8 115.9 %copy-start.2 = (f32[4,128,128]{2,0,1:T(4,128)S(1)}, f32[4,128,128]{2,0,1:T(4,128)}, u32[]{:S(2)}) copy-start(f32[4,128,128]{2,0,1:T(4,128)} %custom-call.2) | copy-start | bytes 786436
  48.8 115.9 %copy-start.5 = (s32[1,16]{1,0:T(1,128)S(1)}, s32[1,16]{1,0:T(1,128)}, u32[]{:S(2)}) copy-start(s32[1,16]{1,0:T(1,128)} %param.23) | copy-start | bytes 196
  278.4 267.9 %all-gather.6.cloned.1.call-start = ((), (), s32[]{:S(2)}) async-start(), calls=%async_computation.1 | async-start | bytes 8519680 | tf_op jit(solution)/shard_map/all_gather | solution.py:61
  319.3 120.0 %copy-start.4 = (bf16[128,128]{1,0:T(8,128)(2,1)S(1)}, bf16[128,128]{1,0:T(8,128)(2,1)}, u32[]{:S(2)}) copy-start(bf16[128,128]{1,0:T(8,128)(2,1)} %param.17) | copy-start | bytes 98308
  440.2 914.0 %all-reduce.8.cloned.1.call-start = ((), (), s32[]{:S(2)}) async-start(), calls=%async_computation.4 | async-start | bytes 262144 | tf_op jit(solution)/shard_map/psum | solution.py:97
  587.2 120.8 %copy-start.3 = (bf16[128,128]{1,0:T(8,128)(2,1)S(1)}, bf16[128,128]{1,0:T(8,128)(2,1)}, u32[]{:S(2)}) copy-start(bf16[128,128]{1,0:T(8,128)(2,1)} %param.18) | copy-start | bytes 98308
Sparse Core Ops, SparseCore 0:
  11.9 110.6 all-gather.7
  125.9 113.1 all-gather.3
  278.5 46.1 all-reduce.5
  440.3 105.9 all-gather.5
  708.0 646.1 all-reduce.7
where the time goes:
time: 1370 us; the launch traced here: 1360 us
  waiting for transfers between devices  824 us (60%)
  local copies, waits for them, and re-layouts  259 us (19%)
  matrix products  141 us (10%)
  other arithmetic  80.6 us (6%)
  blocking collectives  42.8 us (3%)
  between operations  14 us (1%)
    psum x1, waiting for transfers between devices, per_device(): grad_one = lax.psum(row_contract(s_one, d_pre), 'row')  645 us
    all_gather x3, waiting for transfers between devices, propagate(): piece = lax.all_gather(own_block, 'row', axis=0, tiled=True)  178 us
    dynamic_update_slice x3, local copies, waits for them, and re-layouts, propagate(): widened = lax.dynamic_update_slice_in_dim(widened, piece, offset, 0)  117 us
    dot_general x48, matrix products, section_work(): jnp.einsum('mij,mjf->mif', section_tiles, sources, preferred_element_type...  68 us
    dot_general x48, matrix products, section_work(): jnp.einsum('mk,mif->kif', onehot, products, precision=lax.Precision.HIGHEST)  66.7 us
    psum x2, blocking collectives, whole_sum(): return lax.psum(partial_rows, 'rep')  42.8 us
    eq x48, local copies, waits for them, and re-layouts, section_work(): section_rows[:, None] == jnp.arange(count_tiles, dtype=jnp.int32)[None, :]  33.5 us
    and x48, other arithmetic, section_work(): sources = jnp.take(pieces, section_cols, axis=0)  33.4 us
  transfers between devices with their start and end apart: 5, of which 3 were waited for; matrix products, arithmetic and copies ran while one was open for 24% of the time, Pallas kernels for 0%

commit v1 on v0

--- a/solution.py
+++ b/solution.py
@@ -58,7 +58,9 @@
     kept_total = section_total * block_rows
     kept_base = first_section * block_rows
     empty = jnp.zeros((kept_total, width), own_block.dtype)
-    piece = lax.all_gather(own_block, "row", axis=0, tiled=True)
+    piece = jnp.concatenate(
+        lax.all_to_all(jnp.stack([own_block] * lax.axis_size("row")), "row", 0, 0), axis=0
+    )
     piece_rows = piece.shape[0]
     padding = jnp.zeros((piece_rows, width), empty.dtype)
     widened = jnp.concatenate([padding, empty, padding], axis=0)

time: 1370 us -> 1620 us (1.18)
  waiting for transfers between devices: 824 us -> 1020 us
  starting transfers between devices: 0.2 us -> 42.3 us
  local copies, waits for them, and re-layouts: 259 us -> 290 us
    all_to_all x0 -> x3, waiting for transfers between devices: none -> 296 us  [propagate(): lax.all_to_all(jnp.stack([own_block] * lax.axis_size('row')), 'row', 0, 0)]
    all_gather x3 -> x0, waiting for transfers between devices: 178 us -> none  [propagate(): piece = lax.all_gather(own_block, 'row', axis=0, tiled=True)]
    psum x1, waiting for transfers between devices: 0.02 us -> 68 us  [whole_sum(): return lax.psum(partial_rows, 'rep')]
    all_to_all x0 -> x3, starting transfers between devices: none -> 42 us  [propagate(): lax.all_to_all(jnp.stack([own_block] * lax.axis_size('row')), 'row', 0, 0)]
  transfers between devices with their start and end apart: 5 -> 5, of which waited for: 3 -> 5; matrix products, arithmetic and copies ran while one was open for 24% -> 12% of each run, Pallas kernels for 0% -> 0%
where the time goes in v1:
time: 1620 us; the launch traced here: 1610 us
  waiting for transfers between devices  1020 us (63%)
  local copies, waits for them, and re-layouts  290 us (18%)
  matrix products  139 us (9%)
  other arithmetic  80.6 us (5%)
  starting transfers between devices  42.3 us (3%)
  blocking collectives  27.1 us (2%)
    psum x1, waiting for transfers between devices, per_device(): grad_one = lax.psum(row_contract(s_one, d_pre), 'row')  652 us
    all_to_all x3, waiting for transfers between devices, propagate(): lax.all_to_all(jnp.stack([own_block] * lax.axis_size('row')), 'row', 0, 0)  296 us
    dynamic_update_slice x3, local copies, waits for them, and re-layouts, propagate(): widened = lax.dynamic_update_slice_in_dim(widened, piece, offset, 0)  117 us
    psum x1, waiting for transfers between devices, whole_sum(): return lax.psum(partial_rows, 'rep')  68 us
    dot_general x48, matrix products, section_work(): jnp.einsum('mij,mjf->mif', section_tiles, sources, preferred_element_type...  67.9 us
    dot_general x48, matrix products, section_work(): jnp.einsum('mk,mif->kif', onehot, products, precision=lax.Precision.HIGHEST)  66.7 us
    all_to_all x3, starting transfers between devices, propagate(): lax.all_to_all(jnp.stack([own_block] * lax.axis_size('row')), 'row', 0, 0)  42 us
    eq x48, local copies, waits for them, and re-layouts, section_work(): section_rows[:, None] == jnp.arange(count_tiles, dtype=jnp.int32)[None, :]  33.5 us
  transfers between devices with their start and end apart: 5, of which 5 were waited for; matrix products, arithmetic and copies ran while one was open for 12% of the time, Pallas kernels for 0%

profile of v1, /device:TPU:2, one launch (start us, length us, event | category | flops | bytes accessed | tf_op | source)
XLA Modules:
  0.0 1611.4 jit_solution(6650138017145126597)
XLA Ops:
  9.0 5.3 stack.8
  14.3 15.0 all-to-all-start.2
  29.3 186.3 %all-to-all-done.2 = bf16[64,512,128]{2,1,0:T(8,128)(2,1)} async-done(((bf16[64,512,128]{2,1,0:T(8,128)(2,1)}), bf16[64,512,128]{2,1,0:T(8,128)(2,1)}, u32[]{:S(2)}, u32[]{:S(2)}) %all-to-all-start.2) | async-done | bytes 8388640 | tf_op jit(solution)/shard_map/all_to_all | solution.py:62
  215.6 5.3 stack.6
  220.9 7.5 all-to-all-start
  228.4 3.9 broadcast.56
  232.3 15.8 pad_maximum_fusion
  248.1 6.4 copy.46
  254.4 5.7 copy-done.1
  260.2 6.5 copy.38
  266.6 39.0 %dynamic_update_slice.11 = bf16[73728,128]{1,0:T(8,128)(2,1)} dynamic-update-slice(bf16[73728,128]{1,0:T(8,128)(2,1)} %copy.46, bf16[32768,128]{1,0:T(8,128)(2,1)} %bitcast.10, s32[]{:T(128)S(6)} %min.6, s32[]{:T(128)} %constant.163.clone.1) | dynamic-update-slice | bytes 16777220 | tf_op jit(solution)/shard_map/dynamic_update_slice | solution.py:68
  305.7 3.1 slice.20
  308.7 103.9 %all-to-all-done = bf16[64,512,128]{2,1,0:T(8,128)(2,1)} async-done(((bf16[64,512,128]{2,1,0:T(8,128)(2,1)}), bf16[64,512,128]{2,1,0:T(8,128)(2,1)}, u32[]{:S(2)}, u32[]{:S(2)}) %all-to-all-start) | async-done | bytes 8388640 | tf_op jit(solution)/shard_map/all_to_all | solution.py:62
  412.6 39.1 %dynamic_update_slice.9 = bf16[73728,128]{1,0:T(8,128)(2,1)} dynamic-update-slice(bf16[73728,128]{1,0:T(8,128)(2,1)} %copy-done.1, bf16[32768,128]{1,0:T(8,128)(2,1)} %bitcast.3, s32[]{:T(128)S(6)} %min.6, s32[]{:T(128)} %constant.163.clone.1) | dynamic-update-slice | bytes 16777220 | tf_op jit(solution)/shard_map/dynamic_update_slice | solution.py:68
  451.7 3.0 slice.18
  454.8 112.8 %while.42 = (s32[]{:T(128)}, f32[4,128,128]{2,0,1:T(4,128)S(1)}, s32[16]{0:T(128)S(1)}, s32[16,16]{1,0:T(8,128)}, bf16[16,16,128,128]{3,2,1,0:T(8,128)(2,1)}, /*...) while((s32[]{:T(128)}, f32[4,128,128]{2,0,1:T(4,128)S(1)}, ...), condition=%wide.region_1.3_spmd.clone, body=%wide.region_0.2_spmd.clone.sunk | while | flops 80086320 | bytes 4985487 | solution.py:76
  459.0 1.4 fusion.112
  567.6 13.6 all-reduce.9
  581.5 5.3 stack.7
  586.8 19.5 %all-to-all-start.1 = ((bf16[64,512,128]{2,1,0:T(8,128)(2,1)}), bf16[64,512,128]{2,1,0:T(8,128)(2,1)}, u32[]{:S(2)}, u32[]{:S(2)}) async-start(bf16[64,512,128]{2,1,0:T(8,128)(2,1)} %stack.7), calls=%async_computation.1 | async-start | bytes 16777216 | tf_op jit(solution)/shard_map/all_to_all | solution.py:62
  606.5 112.8 %while.44 = (s32[]{:T(128)}, f32[4,128,128]{2,0,1:T(4,128)S(1)}, s32[16]{0:T(128)S(1)}, s32[16,16]{1,0:T(8,128)}, bf16[16,16,128,128]{3,2,1,0:T(8,128)(2,1)}, /*...) while((s32[]{:T(128)}, f32[4,128,128]{2,0,1:T(4,128)S(1)}, ...), condition=%wide.region_7.9_spmd.clone, body=%wide.region_6.8_spmd.clone.sunk | while | flops 80086320 | bytes 4985487 | solution.py:76
  720.2 68.0 %all-reduce.6.cloned.1.call-done = f32[512,128]{1,0:T(8,128)} async-done(((f32[512,128]{1,0:T(8,128)}), f32[512,128]{1,0:T(8,128)}) %all-reduce.6.cloned.1.call-update) | async-done | bytes 262160 | tf_op jit(solution)/shard_map/psum | solution.py:81
  788.2 1.9 fusion.69
  790.1 5.5 all-to-all-done.1
  795.6 39.1 %dynamic_update_slice.10 = bf16[73728,128]{1,0:T(8,128)(2,1)} dynamic-update-slice(bf16[73728,128]{1,0:T(8,128)(2,1)} %copy.38, bf16[32768,128]{1,0:T(8,128)(2,1)} %bitcast.7, s32[]{:T(128)S(6)} %min.6, s32[]{:T(128)} %constant.163.clone.1) | dynamic-update-slice | bytes 16777220 | tf_op jit(solution)/shard_map/dynamic_update_slice | solution.py:68
  834.7 1.7 slice.19
  836.4 98.5 %while.43 = (s32[]{:T(128)}, f32[4,128,128]{2,0,1:T(4,128)S(1)}, s32[16]{0:T(128)S(1)}, s32[16,16]{1,0:T(8,128)}, bf16[16,16,128,128]{3,2,1,0:T(8,128)(2,1)}, /*...) while((s32[]{:T(128)}, f32[4,128,128]{2,0,1:T(4,128)S(1)}, ...), condition=%wide.region_4.6_spmd.clone, body=%wide.region_3.5_spmd.clone.sunk | while | flops 80086320 | bytes 4985487 | solution.py:76
  845.9 1.4 fusion.118
  934.9 13.5 all-reduce.10
  950.1 651.5 %all-reduce.8.cloned.1.call-done = (f32[128,128]{1,0:T(8,128)}, f32[128,128]{1,0:T(8,128)}) async-done(((f32[128,128]{1,0:T(8,128)}, f32[128,128]{1,0:T(8,128)}), (f32[128,128]{1,0:T(8,128)}, f32[128,128]{1,0:T(8,128)})) %all-reduce.8.cloned.1.call-update) | async-done | bytes 131088 | tf_op jit(solution)/shard_map/psum | solution.py:99
  1601.7 1.5 copy.58
  1603.1 1.5 copy.59
  (459 shorter events, 323.9 us)
Async XLA Ops:
  7.2 0.9 copy-start
  14.3 201.3 %copy-start.3 = (bf16[512,128]{1,0:T(8,128)(2,1)S(1)}, bf16[512,128]{1,0:T(8,128)(2,1)}, u32[]{:S(2)}) copy-start(bf16[512,128]{1,0:T(8,128)(2,1)} %param.16) | copy-start | bytes 393220
  14.3 201.3 %all-to-all-start.2 = ((bf16[64,512,128]{2,1,0:T(8,128)(2,1)}), bf16[64,512,128]{2,1,0:T(8,128)(2,1)}, u32[]{:S(2)}, u32[]{:S(2)}) async-start(bf16[64,512,128]{2,1,0:T(8,128)(2,1)} %stack.8), calls=%async_computation.2 | async-start | bytes 16777216 | tf_op jit(solution)/shard_map/all_to_all | solution.py:62
  220.9 191.7 %all-to-all-start = ((bf16[64,512,128]{2,1,0:T(8,128)(2,1)}), bf16[64,512,128]{2,1,0:T(8,128)(2,1)}, u32[]{:S(2)}, u32[]{:S(2)}) async-start(bf16[64,512,128]{2,1,0:T(8,128)(2,1)} %stack.6), calls=%async_computation | async-start | bytes 16777216 | tf_op jit(solution)/shard_map/all_to_all | solution.py:62
  248.1 12.1 copy-start.1
  412.6 42.1 %copy-start.2 = (f32[4,128,128]{2,0,1:T(4,128)S(1)}, f32[4,128,128]{2,0,1:T(4,128)}, u32[]{:S(2)}) copy-start(f32[4,128,128]{2,0,1:T(4,128)} %custom-call) | copy-start | bytes 786436
  412.6 42.1 %copy-start.6 = (s32[1,16]{1,0:T(1,128)S(1)}, s32[1,16]{1,0:T(1,128)}, u32[]{:S(2)}) copy-start(s32[1,16]{1,0:T(1,128)} %param.23) | copy-start | bytes 196
  454.8 126.5 %copy-start.5 = (bf16[128,128]{1,0:T(8,128)(2,1)S(1)}, bf16[128,128]{1,0:T(8,128)(2,1)}, u32[]{:S(2)}) copy-start(bf16[128,128]{1,0:T(8,128)(2,1)} %param.17) | copy-start | bytes 98308
  586.8 208.8 %all-to-all-start.1 = ((bf16[64,512,128]{2,1,0:T(8,128)(2,1)}), bf16[64,512,128]{2,1,0:T(8,128)(2,1)}, u32[]{:S(2)}, u32[]{:S(2)}) async-start(bf16[64,512,128]{2,1,0:T(8,128)(2,1)} %stack.7), calls=%async_computation.1 | async-start | bytes 16777216 | tf_op jit(solution)/shard_map/all_to_all | solution.py:62
  606.3 181.9 %all-reduce.6.cloned.1.call-start = ((), (), s32[]{:S(2)}) async-start(), calls=%async_computation.3 | async-start | bytes 524288 | tf_op jit(solution)/shard_map/psum | solution.py:81
  720.1 881.5 %all-reduce.8.cloned.1.call-start = ((), (), s32[]{:S(2)}) async-start(), calls=%async_computation.4 | async-start | bytes 262144 | tf_op jit(solution)/shard_map/psum | solution.py:99
  836.4 112.9 %copy-start.4 = (bf16[128,128]{1,0:T(8,128)(2,1)S(1)}, bf16[128,128]{1,0:T(8,128)(2,1)}, u32[]{:S(2)}) copy-start(bf16[128,128]{1,0:T(8,128)(2,1)} %param.18) | copy-start | bytes 98308
Sparse Core Ops, SparseCore 0:
  720.2 67.9 all-reduce.5
  949.4 652.1 all-reduce.7
